TPU v7x, 128 devices: a whole 4x4x4 slice. The times are simulated.
128 devices in a mesh: grp: 8 (over z, x_hi), dev: 16 (over y, x_lo, core).
Axes of the slice: x: 4 (x_hi: 2, x_lo: 2; x = x_hi * 2 + x_lo), y: 4, z: 4, core: 2. Of those that a mesh axis runs over, the one named last changes fastest.
Arguments:
- output_gradient: bfloat16 [16384, 2048], P(('grp', 'dev')), may hold values from -6 to 6
- expert_choice_index: int32 [16384, 8], P(('grp', 'dev')), may hold values from 0 to 127, all different within a row; in each aligned block of 128 rows (0 to 127, 128 to 255, ...) at most 10 rows name the same one
- routing_weight: float32 [16384, 8], P(('grp', 'dev')), may hold values from 0.05 to 0.3
- stored_gate_preact: bfloat16 [128, 1280, 1536], P(('grp', 'dev')), may hold values from -6 to 6
- gate_up_weight: bfloat16 [128, 2048, 1536], P(('grp', 'dev')), may hold values from -0.125 to 0.125
- down_weight: bfloat16 [128, 768, 2048], P(('grp', 'dev')), may hold values from -0.21875 to 0.21875
- down_first_factor: bfloat16 [128, 64, 768], P(('grp', 'dev')), may hold values from -0.21875 to 0.21875
- down_second_factor: bfloat16 [128, 64, 2048], P(('grp', 'dev')), may hold values from -0.75 to 0.75
- rotated_queries: bfloat16 [16384, 4096], P('grp', 'dev'), may hold values from -800 to 800
- rotated_keys: bfloat16 [16384, 512], P('grp'), may hold values from -4 to 4
- stored_values: bfloat16 [16384, 512], P('grp'), may hold values from -6 to 6
- output_weight: bfloat16 [4096, 2048], P('dev'), may hold values from -0.09375 to 0.09375
- output_first_factor: bfloat16 [64, 4096], P(None, 'dev'), may hold values from -0.09375 to 0.09375
- output_second_factor: bfloat16 [64, 2048], replicated, may hold values from -0.75 to 0.75
Outputs:
- first_factor_gradient: float32 [128, 64, 768], P(('grp', 'dev'))
- second_factor_gradient: float32 [128, 64, 2048], P(('grp', 'dev'))
- residual_gradient: bfloat16 [16384, 2048], P(('grp', 'dev'))
- output_first_gradient: float32 [64, 4096], P(None, 'dev')
- output_second_gradient: float32 [64, 2048], replicated
- query_gradient: float32 [16384, 4096], P('grp', 'dev')
- key_gradient: float32 [16384, 512], P(('grp', 'dev'))
- value_gradient: float32 [16384, 512], P(('grp', 'dev'))
Inputs may be any that keep to these rules, and one draw needn't show every extreme that they name: `expert_choice_index`: each row names 8 different experts; within the rows of one device no expert is named more than 10 times, a bound that some block reaches.
All inputs are finite; a program needn't handle non-finite values.
Results may differ from a plain program's by a relative error of at most 0.024.
Values may be sent and summed in bfloat16 or wider, within the bound.
A program may use at most 192 MiB of HBM per device.

v0:
```python
import jax
import jax.numpy as jnp
from jax import lax
from jax.sharding import PartitionSpec as P

QUERY_HEADS = 32
KVH = 4
HEAD_SIZE = 128
adapter_scale = 2.0
neg_big = -1e30


def contraction(left, right, left_dim, right_dim):
    return lax.dot_general(
        left, right, (((left_dim,), (right_dim,)), ((), ())), preferred_element_type=jnp.float32
    )


def expert_backward(routed_rows, saved_rows, gate_up, down_output, lowrank_first, low_b):
    width_ff = down_output.shape[0]
    pre_gate = saved_rows[:, :width_ff].astype(jnp.float32)
    pre_up = saved_rows[:, width_ff:].astype(jnp.float32)
    sigmoid = jax.nn.sigmoid(pre_gate)
    activated = pre_gate * sigmoid
    slope = sigmoid * (1.0 + pre_gate * (1.0 - sigmoid))
    hidden_activity = (activated * pre_up).astype(jnp.bfloat16)
    lowrank_input = contraction(hidden_activity, lowrank_first, 1, 1).astype(jnp.bfloat16)
    lowrank_gradient = contraction(routed_rows, low_b, 1, 1).astype(jnp.bfloat16)
    gradient_second = adapter_scale * contraction(lowrank_input, routed_rows, 0, 0)
    gradient_first = adapter_scale * contraction(lowrank_gradient, hidden_activity, 0, 0)
    hidden_gradient = contraction(routed_rows, down_output, 1, 1) + adapter_scale * jnp.dot(
        lowrank_gradient, lowrank_first, preferred_element_type=jnp.float32
    )
    grad_pre = jnp.concatenate(
        [hidden_gradient * pre_up * slope, hidden_gradient * activated], axis=1
    ).astype(jnp.bfloat16)
    return (
        contraction(grad_pre, gate_up, 1, 1).astype(jnp.bfloat16),
        gradient_first,
        gradient_second,
    )


def on_device(
    output_gradient,
    expert_choice_index,
    routing_weight,
    stored_gate_preact,
    gate_up_weight,
    down_weight,
    down_first_factor,
    down_second_factor,
    rotated_queries,
    rotated_keys,
    stored_values,
    output_weight,
    output_first_factor,
    output_second_factor,
):
    tok_rows, model_width = output_gradient.shape
    top_count = expert_choice_index.shape[1]
    grp_count = lax.axis_size("grp")
    dev_count = lax.axis_size("dev")
    experts = grp_count * dev_count
    slot_count = stored_gate_preact.shape[1]
    capacity = slot_count // experts
    assign = tok_rows * top_count
    flat_ids = expert_choice_index.reshape(assign)
    onehot = (flat_ids[:, None] == jnp.arange(experts, dtype=jnp.int32)[None, :]).astype(jnp.int32)
    before = jnp.cumsum(onehot, axis=0) - onehot
    slot_rank = jnp.sum(before * onehot, axis=1)
    cells = flat_ids * capacity + slot_rank
    scaled = (
        (routing_weight[:, :, None] * output_gradient[:, None, :].astype(jnp.float32))
        .astype(jnp.bfloat16)
        .reshape(assign, model_width)
    )
    outgoing = jnp.zeros((experts * capacity, model_width), jnp.bfloat16).at[cells].set(scaled)
    outgoing = outgoing.reshape(experts, capacity, model_width)
    incoming = lax.all_to_all(outgoing, ("grp", "dev"), split_axis=0, concat_axis=0, tiled=True)
    routed_rows = incoming.reshape(slot_count, model_width)
    grad_rows, gradient_first, gradient_second = expert_backward(
        routed_rows,
        stored_gate_preact[0],
        gate_up_weight[0],
        down_weight[0],
        down_first_factor[0],
        down_second_factor[0],
    )
    returned = lax.all_to_all(
        grad_rows.reshape(experts, capacity, model_width),
        ("grp", "dev"),
        split_axis=0,
        concat_axis=0,
        tiled=True,
    )
    picked = returned.reshape(experts * capacity, model_width)[cells]
    merged_result = jnp.sum(
        picked.reshape(tok_rows, top_count, model_width).astype(jnp.float32), axis=1
    )
    residual_gradient = (output_gradient.astype(jnp.float32) + merged_result).astype(jnp.bfloat16)
    segment_gradient = lax.all_gather(residual_gradient, "dev", axis=0, tiled=True)
    piece_len = segment_gradient.shape[0]
    device_share = rotated_queries.shape[1] // HEAD_SIZE
    group_size = QUERY_HEADS // KVH
    rank_total = output_second_factor.shape[0]
    kv_index = lax.axis_index("dev") * device_share // group_size
    key_rows = lax.dynamic_slice_in_dim(rotated_keys, kv_index * HEAD_SIZE, HEAD_SIZE, 1)
    value_rows = lax.dynamic_slice_in_dim(stored_values, kv_index * HEAD_SIZE, HEAD_SIZE, 1)
    lowrank_token = contraction(segment_gradient, output_second_factor, 1, 1).astype(jnp.bfloat16)
    head_gradient = (
        contraction(segment_gradient, output_weight, 1, 1)
        + adapter_scale
        * jnp.dot(lowrank_token, output_first_factor, preferred_element_type=jnp.float32)
    ).astype(jnp.bfloat16)
    lowrank_heads = output_first_factor.reshape(rank_total, device_share, HEAD_SIZE)
    att_scale = HEAD_SIZE ** (-0.5)
    block_rows = min(512, piece_len)
    grad_key_sum = jnp.zeros((piece_len, HEAD_SIZE), jnp.float32)
    grad_value_sum = jnp.zeros((piece_len, HEAD_SIZE), jnp.float32)
    row_contrib = jnp.zeros((rank_total, device_share * HEAD_SIZE), jnp.float32)
    column_contrib = jnp.zeros((rank_total, model_width), jnp.float32)
    query_parts = []
    for number in range(piece_len // block_rows):
        first_row = number * block_rows
        last_row = first_row + block_rows
        query_block = rotated_queries[first_row:last_row].reshape(
            block_rows, device_share, HEAD_SIZE
        )
        grad_block = head_gradient[first_row:last_row].reshape(block_rows, device_share, HEAD_SIZE)
        key_part = key_rows[:last_row]
        value_part = value_rows[:last_row]
        scores = (
            jnp.einsum("qhd,kd->hqk", query_block, key_part, preferred_element_type=jnp.float32)
            * att_scale
        )
        positions = first_row + jnp.arange(block_rows, dtype=jnp.int32)
        causal = positions[:, None] >= jnp.arange(last_row, dtype=jnp.int32)[None, :]
        scores = jnp.where(causal[None, :, :], scores, neg_big)
        probs_full = jnp.exp(scores - jnp.max(scores, axis=2, keepdims=True))
        probs_full = probs_full / jnp.sum(probs_full, axis=2, keepdims=True)
        probs_low = probs_full.astype(jnp.bfloat16)
        attended = jnp.einsum(
            "hqk,kd->qhd", probs_low, value_part, preferred_element_type=jnp.float32
        ).astype(jnp.bfloat16)
        grad_probs = jnp.einsum(
            "qhd,kd->hqk", grad_block, value_part, preferred_element_type=jnp.float32
        )
        row_delta = jnp.sum(grad_block.astype(jnp.float32) * attended.astype(jnp.float32), axis=2)
        grad_scores = (probs_full * (grad_probs - row_delta.T[:, :, None])).astype(jnp.bfloat16)
        query_parts.append(
            att_scale
            * jnp.einsum("hqk,kd->qhd", grad_scores, key_part, preferred_element_type=jnp.float32)
        )
        grad_key_sum = grad_key_sum.at[:last_row].add(
            att_scale
            * jnp.einsum(
                "hqk,qhd->kd", grad_scores, query_block, preferred_element_type=jnp.float32
            )
        )
        grad_value_sum = grad_value_sum.at[:last_row].add(
            jnp.einsum("hqk,qhd->kd", probs_low, grad_block, preferred_element_type=jnp.float32)
        )
        row_contrib = row_contrib + contraction(
            lowrank_token[first_row:last_row],
            attended.reshape(block_rows, device_share * HEAD_SIZE),
            0,
            0,
        )
        flattened = jnp.einsum(
            "qhd,rhd->qhr", attended, lowrank_heads, preferred_element_type=jnp.float32
        ).astype(jnp.bfloat16)
        column_contrib = column_contrib + jnp.einsum(
            "qhr,qc->rc",
            flattened,
            segment_gradient[first_row:last_row],
            preferred_element_type=jnp.float32,
        )
    query_gradient = jnp.concatenate(query_parts, axis=0).reshape(
        piece_len, device_share * HEAD_SIZE
    )
    output_first_gradient = lax.psum(
        (adapter_scale * row_contrib).astype(jnp.bfloat16), "grp"
    ).astype(jnp.float32)
    output_second_gradient = lax.psum(adapter_scale * column_contrib, ("grp", "dev"))
    empty = jnp.zeros((piece_len, KVH * HEAD_SIZE), jnp.float32)
    key_term = lax.dynamic_update_slice(empty, grad_key_sum, (0, kv_index * HEAD_SIZE))
    value_term = lax.dynamic_update_slice(empty, grad_value_sum, (0, kv_index * HEAD_SIZE))
    key_gradient, value_gradient = (
        lax.psum_scatter(
            key_term.astype(jnp.bfloat16), "dev", scatter_dimension=0, tiled=True
        ).astype(jnp.float32),
        lax.psum_scatter(
            value_term.astype(jnp.bfloat16), "dev", scatter_dimension=0, tiled=True
        ).astype(jnp.float32),
    )
    return (
        gradient_first[None],
        gradient_second[None],
        residual_gradient,
        output_first_gradient,
        output_second_gradient,
        query_gradient,
        key_gradient,
        value_gradient,
    )


def solution(mesh):
    in_specs = (
        P(("grp", "dev"), None),
        P(("grp", "dev"), None),
        P(("grp", "dev"), None),
        P(("grp", "dev"), None, None),
        P(("grp", "dev"), None, None),
        P(("grp", "dev"), None, None),
        P(("grp", "dev"), None, None),
        P(("grp", "dev"), None, None),
        P("grp", "dev"),
        P("grp", None),
        P("grp", None),
        P("dev", None),
        P(None, "dev"),
        P(),
    )
    out_specs = (
        P(("grp", "dev"), None, None),
        P(("grp", "dev"), None, None),
        P(("grp", "dev"), None),
        P(None, "dev"),
        P(),
        P("grp", "dev"),
        P(("grp", "dev"), None),
        P(("grp", "dev"), None),
    )
    return jax.shard_map(
        on_device, mesh=mesh, in_specs=in_specs, out_specs=out_specs, check_vma=False
    )
```

profile of v0, /device:TPU:1, one launch (start us, length us, event | category | flops | bytes accessed | tf_op | source)
XLA Modules:
  0.0 718.6 jit_solution(16234337022996242933)
XLA Ops:
  12.4 2.1 convert_element_type.174
  14.7 1.4 fusion.100
  16.2 10.5 %scatter_custom_fusion = bf16[1280,2048]{1,0:T(8,128)(2,1)} fusion(s32[1024]{0:T(1024)S(1)} %bitcast.379, f32[128,2048]{1,0:T(8,128)} %convert_element_type.174, f32[1024]{0:T(1024)S(1)} %mul.209, bf16[]{:T(256)} %constant.250.clone.1), kind=kCustom, calls=%fused_computation.28 | custom fusion | flops 4194304 | bytes 6295554 | tf_op jit(solution)/shard_map/scatter | solution.py:78
  26.6 9.5 %reshape.411 = bf16[128,10,2048]{2,1,0:T(8,128)(2,1)} reshape(bf16[1280,2048]{1,0:T(8,128)(2,1)} %scatter_custom_fusion) | data formatting | bytes 10485760 | tf_op jit(solution)/shard_map/reshape | solution.py:79
  36.2 12.4 %all-to-all-start = ((bf16[128,10,2048]{2,1,0:T(8,128)(2,1)}), bf16[128,10,2048]{2,1,0:T(8,128)(2,1)}, u32[]{:S(2)}, u32[]{:S(2)}) async-start(bf16[128,10,2048]{2,1,0:T(8,128)(2,1)} %reshape.411), calls=%async_computation | async-start | bytes 16777216 | tf_op jit(solution)/shard_map/all_to_all | solution.py:80
  48.6 6.2 copy.100
  54.9 94.9 %all-to-all-done = bf16[128,10,2048]{2,1,0:T(8,128)(2,1)} async-done(((bf16[128,10,2048]{2,1,0:T(8,128)(2,1)}), bf16[128,10,2048]{2,1,0:T(8,128)(2,1)}, u32[]{:S(2)}, u32[]{:S(2)}) %all-to-all-start) | async-done | bytes 5242912 | tf_op jit(solution)/shard_map/all_to_all | solution.py:80
  149.8 9.8 %reshape.412 = bf16[1280,2048]{1,0:T(8,128)(2,1)} reshape(bf16[128,10,2048]{2,1,0:T(8,128)(2,1)} %all-to-all-done) | data formatting | bytes 10485760 | tf_op jit(solution)/shard_map/reshape | solution.py:81
  159.6 4.3 convolution_convert_fusion.3
  164.0 4.3 fusion.35
  168.3 3.8 fusion.24
  172.2 10.2 %convolution_convert_fusion = bf16[1280,2048]{1,0:T(8,128)(2,1)} fusion(bf16[1,2048,1536]{2,1,0:T(8,128)(2,1)S(1)} %bitcast.382, bf16[1280,768]{0,1:T(8,128)(2,1)S(1)} %get-tuple-element.149, bf16[1280,768]{0,1:T(8,128)(2,1)S(1)} %get-tuple-element.148), kind=kOutput, calls=%fused_computation.14 | convolution fusion | flops 8063549440 | bytes 15466496 | tf_op jit(solution)/shard_map/dot_general | solution.py:14
  182.4 9.5 %reshape.413 = bf16[128,10,2048]{2,1,0:T(8,128)(2,1)} reshape(bf16[1280,2048]{1,0:T(8,128)(2,1)} %convolution_convert_fusion) | data formatting | bytes 10485760 | tf_op jit(solution)/shard_map/reshape | solution.py:91
  191.9 15.0 %all-to-all-start.1 = ((bf16[128,10,2048]{2,1,0:T(8,128)(2,1)}), bf16[128,10,2048]{2,1,0:T(8,128)(2,1)}, u32[]{:S(2)}, u32[]{:S(2)}) async-start(bf16[128,10,2048]{2,1,0:T(8,128)(2,1)} %reshape.413), calls=%async_computation.1 | async-start | bytes 16777216 | tf_op jit(solution)/shard_map/all_to_all | solution.py:90
  206.9 101.3 %all-to-all-done.1 = bf16[128,10,2048]{2,1,0:T(8,128)(2,1)} async-done(((bf16[128,10,2048]{2,1,0:T(8,128)(2,1)}), bf16[128,10,2048]{2,1,0:T(8,128)(2,1)}, u32[]{:S(2)}, u32[]{:S(2)}) %all-to-all-start.1) | async-done | bytes 5242912 | tf_op jit(solution)/shard_map/all_to_all | solution.py:90
  308.2 9.8 %reshape.414 = bf16[1280,2048]{1,0:T(8,128)(2,1)} reshape(bf16[128,10,2048]{2,1,0:T(8,128)(2,1)} %all-to-all-done.1) | data formatting | bytes 10485760 | tf_op jit(solution)/shard_map/reshape | solution.py:97
  318.1 12.0 %gather_fusion = bf16[1024,2048]{1,0:T(8,128)(2,1)} fusion(bf16[1280,2048]{1,0:T(8,128)(2,1)} %reshape.414, s32[1024]{0:T(1024)S(1)} %broadcast_clamp_fusion), kind=kCustom, calls=%fused_computation | custom fusion | bytes 8392704 | tf_op jit(solution)/shard_map/gather | solution.py:97
  330.0 5.1 convert_reduce_fusion
  336.1 8.8 %reduce-scatter.3.cloned.1.call-start = ((), (), s32[]{:S(2)}) async-start(), calls=%async_computation.6 | async-start | bytes 2228224 | tf_op jit(solution)/shard_map/reduce_scatter | solution.py:190
  351.5 4.6 fusion.177
  356.0 2.9 fusion.67
  358.9 1.4 convolution_convert_fusion.5
  360.3 3.2 fusion.176
  364.1 6.1 fusion.178
  370.2 3.8 fusion.43
  374.0 1.3 convolution_convert_fusion.4
  375.8 1.3 fusion.96
  377.1 1.8 iota_compare_fusion
  378.9 8.2 %fusion.179 = (f32[2,512]{1,0:T(2,128)S(1)}, f32[2,512,2048]{1,2,0:T(8,128)}) fusion(pred[512,2048]{0,1:T(8,128)(4,1)} %iota_compare_fusion, bf16[512,2,128]{0,2,1:T(8,128)(2,1)S(1)} %bitcast.363, bf16[2048,512]{1,0:T(8,128)(2,1)} %param.43, s32[]{:T(128)S(6)} %select_n.40), kind=kOutput, calls=%fused_computation.246 | convolution fusion | flops 545261568 | bytes 10227716 | tf_op jit(solution)/shard_map/sub | solution.py:140
  387.1 4.7 fusion.33
  391.8 2.0 copy-done.2
  394.6 6.1 fusion.184
  400.8 2.6 convolution_convert_fusion.2
  409.3 1.2 fusion.5
  412.2 3.0 copy-done.20
  415.2 1.2 fusion.15
  418.6 1.5 broadcast_in_dim.100.clone
  420.1 2.1 fusion.46
  422.3 1.9 fusion.83
  424.2 1.8 fusion.81
  426.1 1.7 convolution_bitcast_fusion.6
  430.9 1.5 fusion.53
  432.4 1.3 copy-done.14
  433.8 3.0 fusion.86
  436.7 5.4 fusion.54
  442.1 1.3 fusion.137
  443.5 1.2 convolution_add_fusion.5
  444.7 1.2 convolution_add_fusion.4
  446.9 38.8 %psum.14 = bf16[64,256]{1,0:T(8,128)(2,1)S(1)} all-reduce(bf16[64,256]{1,0:T(8,128)(2,1)S(1)} %fusion.88), channel_id=1, replica_groups=mesh['grp'=8,'dev'=16] {'grp'}, use_global_device_ids=true, to_apply=%region_13.14 | all-reduce | flops 16384 | bytes 65536 | tf_op jit(solution)/shard_map/psum | solution.py:182
  487.5 2.0 fusion.69
  489.6 2.3 fusion.74
  491.8 2.1 fusion.59
  493.9 2.1 convolution_add_fusion.2
  496.0 2.2 convolution_add_fusion.1
  498.2 2.9 fusion.55
  501.1 2.6 fusion.68
  503.7 2.6 fusion.73
  506.4 3.2 pad_maximum_fusion
  509.6 2.9 copy.142
  512.5 1.6 convert_element_type.222
  514.1 42.5 %reduce-scatter.5.cloned.1.call-done = bf16[128,512]{1,0:T(8,128)(2,1)} async-done(((bf16[2048,512]{1,0:T(8,128)(2,1)}), bf16[128,512]{1,0:T(8,128)(2,1)}) %reduce-scatter.5.cloned.1.call-update) | async-done | bytes 131088 | tf_op jit(solution)/shard_map/reduce_scatter | solution.py:193
  556.6 1.6 convert_element_type.224
  558.2 151.8 %all-reduce.4.cloned.1.call-done = f32[64,2048]{1,0:T(8,128)} async-done(((f32[64,2048]{1,0:T(8,128)}), f32[64,2048]{1,0:T(8,128)}) %all-reduce.4.cloned.1.call-update) | async-done | bytes 524304 | tf_op jit(solution)/shard_map/psum | solution.py:185
  710.0 1.9 copy.217
  (197 shorter events, 30.4 us)
Async XLA Ops:
  7.2 156.8 %copy-start = (bf16[1,768,2048]{2,1,0:T(8,128)(2,1)S(1)}, bf16[1,768,2048]{2,1,0:T(8,128)(2,1)}, u32[]{:S(2)}) copy-start(bf16[1,768,2048]{2,1,0:T(8,128)(2,1)} %param.39) | copy-start | bytes 9437188
  7.2 7.4 %copy-start.60 = (f32[128,8]{0,1:T(8,128)S(1)}, f32[128,8]{0,1:T(8,128)}, u32[]{:S(2)}) copy-start(f32[128,8]{0,1:T(8,128)} %param.36) | copy-start | bytes 12292
  36.2 113.6 %all-to-all-start = ((bf16[128,10,2048]{2,1,0:T(8,128)(2,1)}), bf16[128,10,2048]{2,1,0:T(8,128)(2,1)}, u32[]{:S(2)}, u32[]{:S(2)}) async-start(bf16[128,10,2048]{2,1,0:T(8,128)(2,1)} %reshape.411), calls=%async_computation | async-start | bytes 16777216 | tf_op jit(solution)/shard_map/all_to_all | solution.py:80
  54.9 104.8 %copy-start.53 = (bf16[1,64,2048]{2,1,0:T(8,128)(2,1)S(1)}, bf16[1,64,2048]{2,1,0:T(8,128)(2,1)}, u32[]{:S(2)}) copy-start(bf16[1,64,2048]{2,1,0:T(8,128)(2,1)} %param.41) | copy-start | bytes 786436
  159.6 4.4 copy-start.4
  164.0 4.3 copy-start.51
  164.0 4.3 copy-start.22
  164.0 4.3 copy-start.59
  164.0 8.1 %slice-start.4 = ((s8[6291456]{0:T(1024)(128)(4,1)}), s8[4194304]{0:T(1024)(128)(4,1)S(1)}, s32[]{:S(2)}) async-start(s8[6291456]{0:T(1024)(128)(4,1)} %bitcast.381), calls=%async_computation.12 | async-start | bytes 8388608
  168.3 3.8 slice-start.5
  191.9 116.3 %all-to-all-start.1 = ((bf16[128,10,2048]{2,1,0:T(8,128)(2,1)}), bf16[128,10,2048]{2,1,0:T(8,128)(2,1)}, u32[]{:S(2)}, u32[]{:S(2)}) async-start(bf16[128,10,2048]{2,1,0:T(8,128)(2,1)} %reshape.413), calls=%async_computation.1 | async-start | bytes 16777216 | tf_op jit(solution)/shard_map/all_to_all | solution.py:90
  206.9 187.7 %all-gather.2.cloned.1.call-start = ((), (), s32[]{:S(2)}) async-start(), calls=%async_computation.4 | async-start | bytes 8912896 | tf_op jit(solution)/shard_map/all_gather | solution.py:102
  330.0 5.1 copy-start.29
  335.1 11.0 %copy-start.38 = (bf16[2048,256]{1,0:T(8,128)(2,1)S(1)}, bf16[2048,256]{1,0:T(8,128)(2,1)}, u32[]{:S(2)}) copy-start(bf16[2048,256]{1,0:T(8,128)(2,1)} %param.42) | copy-start | bytes 3145732
  336.1 176.4 %reduce-scatter.3.cloned.1.call-start = ((), (), s32[]{:S(2)}) async-start(), calls=%async_computation.6 | async-start | bytes 2228224 | tf_op jit(solution)/shard_map/reduce_scatter | solution.py:190
  346.0 5.4 copy-start.15
  348.0 8.0 %copy-start.45 = (bf16[512,256]{0,1:T(8,128)(2,1)}, bf16[512,256]{0,1:T(8,128)(2,1)S(1)}, u32[]{:S(2)}) copy-start(bf16[512,256]{0,1:T(8,128)(2,1)S(1)} %copy.185) | copy-start | bytes 786436
  348.1 10.8 %copy-start.36 = (bf16[1024,128]{0,1:T(8,128)(2,1)}, bf16[1024,128]{0,1:T(8,128)(2,1)S(1)}, u32[]{:S(2)}) copy-start(bf16[1024,128]{0,1:T(8,128)(2,1)S(1)} %copy.189) | copy-start | bytes 786436
  348.3 15.8 %copy-start.32 = (bf16[512,256]{0,1:T(8,128)(2,1)}, bf16[512,256]{0,1:T(8,128)(2,1)S(1)}, u32[]{:S(2)}) copy-start(bf16[512,256]{0,1:T(8,128)(2,1)S(1)} %copy.186) | copy-start | bytes 786436
  348.5 25.5 %copy-start.30 = (bf16[1536,128]{0,1:T(8,128)(2,1)}, bf16[1536,128]{0,1:T(8,128)(2,1)S(1)}, u32[]{:S(2)}) copy-start(bf16[1536,128]{0,1:T(8,128)(2,1)S(1)} %copy.190) | copy-start | bytes 1179652
  349.5 10.8 %copy-start.39 = (bf16[512,256]{0,1:T(8,128)(2,1)}, bf16[512,256]{0,1:T(8,128)(2,1)S(1)}, u32[]{:S(2)}) copy-start(bf16[512,256]{0,1:T(8,128)(2,1)S(1)} %copy.184) | copy-start | bytes 786436
  356.0 4.3 copy-start.55
  358.9 11.3 %copy-start.10 = (bf16[2,512,1024]{1,2,0:T(8,128)(2,1)}, bf16[2,512,1024]{1,2,0:T(8,128)(2,1)S(1)}, u32[]{:S(2)}) copy-start(bf16[2,512,1024]{1,2,0:T(8,128)(2,1)S(1)} %fusion.67) | copy-start | bytes 6291460
  374.0 1.8 copy-start.27
  375.3 3.6 copy-start.34
  387.1 6.7 copy-start.16
  391.8 2.0 copy-start.2
  394.6 6.2 copy-start.5
  394.6 6.2 copy-start.54
  400.8 2.7 copy-start.50
  403.5 2.6 copy-start.23
  403.5 1.4 copy-start.58
  403.5 2.6 copy-start.28
  404.0 4.3 slice-start
  405.0 1.7 copy-start.47
  405.0 3.4 copy-start.41
  405.0 5.6 copy-start.43
  405.0 7.3 %copy-start.48 = (bf16[512,256]{0,1:T(8,128)(2,1)}, bf16[512,256]{0,1:T(8,128)(2,1)S(1)}, u32[]{:S(2)}) copy-start(bf16[512,256]{0,1:T(8,128)(2,1)S(1)} %get-tuple-element.154) | copy-start | bytes 786436
  406.1 3.1 slice-start.1
  406.1 3.1 copy-start.17
  407.3 3.2 slice-start.2
  409.3 1.9 slice-start.3
  409.3 1.9 copy-start.31
  410.5 9.6 %copy-start.6 = (bf16[2,512,2048]{1,2,0:T(8,128)(2,1)}, bf16[2,512,2048]{1,2,0:T(8,128)(2,1)S(1)}, u32[]{:S(2)}) copy-start(bf16[2,512,2048]{1,2,0:T(8,128)(2,1)S(1)} %fusion.5) | copy-start | bytes 12582916
  411.2 4.0 copy-start.20
  411.2 4.0 copy-start.37
  412.2 5.1 copy-start.8
  416.4 2.2 copy-start.12
  417.6 2.5 copy-start.35
  422.2 134.4 %reduce-scatter.5.cloned.1.call-start = ((), (), s32[]{:S(2)}) async-start(), calls=%async_computation.7 | async-start | bytes 2228224 | tf_op jit(solution)/shard_map/reduce_scatter | solution.py:193
  422.3 5.7 copy-start.11
  422.3 5.7 copy-start.49
  422.3 6.4 copy-start.44
  428.7 2.2 copy-start.3
  428.7 2.2 copy-start.42
  430.9 2.9 copy-start.52
  433.7 276.3 %all-reduce.4.cloned.1.call-start = ((), (), s32[]{:S(2)}) async-start(), calls=%async_computation.5 | async-start | bytes 1048576 | tf_op jit(solution)/shard_map/psum | solution.py:185
  436.7 50.8 %copy-start.19 = (bf16[2,512,512]{1,2,0:T(8,128)(2,1)S(1)}, bf16[2,512,512]{1,2,0:T(8,128)(2,1)}, u32[]{:S(2)}) copy-start(bf16[2,512,512]{1,2,0:T(8,128)(2,1)} %copy-done.18) | copy-start | bytes 3145732
  442.1 47.4 %copy-start.13 = (bf16[2,512,1024]{1,2,0:T(8,128)(2,1)S(1)}, bf16[2,512,1024]{1,2,0:T(8,128)(2,1)}, u32[]{:S(2)}) copy-start(bf16[2,512,1024]{1,2,0:T(8,128)(2,1)} %copy-done.12) | copy-start | bytes 6291460
  446.9 47.0 %copy-start.57 = (bf16[512,64]{0,1:T(8,128)(2,1)S(1)}, bf16[512,64]{0,1:T(8,128)(2,1)}, u32[]{:S(2)}) copy-start(bf16[512,64]{0,1:T(8,128)(2,1)} %fusion.83) | copy-start | bytes 196612
  489.6 6.4 copy-start.56
  496.0 5.1 copy-start.9
  501.1 2.6 copy-start.7
  506.4 205.6 %copy-start.1 = (bf16[1,768,2048]{2,1,0:T(8,128)(2,1)S(1)}, bf16[1,768,2048]{2,1,0:T(8,128)(2,1)}, u32[]{:S(2)}) copy-start(bf16[1,768,2048]{2,1,0:T(8,128)(2,1)} %param.39) | copy-start | bytes 9437188
  (9 other events, 10.8 us)
Sparse Core Ops, SparseCore 0:
  336.2 57.9 all-gather.1
  422.3 67.4 reduce-scatter.2
  492.3 64.2 reduce-scatter.4
  561.8 148.2 all-reduce.3
where the time goes:
time: 727 us; the launch traced here: 719 us
  waiting for transfers between devices  391 us (54%)
  matrix products  108 us (15%)
  local copies, waits for them, and re-layouts  84 us (12%)
  other arithmetic  45.6 us (6%)
  blocking collectives  38.8 us (5%)
  starting transfers between devices  36.4 us (5%)
  between operations  14.9 us (2%)
    psum x1, waiting for transfers between devices, on_device(): lax.psum(adapter_scale * column_contrib, ('grp', 'dev'))  152 us
    all_to_all x1, waiting for transfers between devices, on_device(): lax.all_to_all(grad_rows.reshape(experts, capacity, model_width), ('grp',...  101 us
    all_to_all x1, waiting for transfers between devices, on_device(): lax.all_to_all(outgoing, ('grp', 'dev'), split_axis=0, concat_axis=0, til...  94.9 us
    reduce_scatter x1, waiting for transfers between devices, on_device(): lax.psum_scatter(value_term.astype(jnp.bfloat16), 'dev', scatter_dimensio...  42.5 us
    dot_general x11, matrix products, contraction(): lax.dot_general(left, right, (((left_dim,), (right_dim,)), ((), ())), pre...  40.8 us
    psum x1, blocking collectives, on_device(): lax.psum((adapter_scale * row_contrib).astype(jnp.bfloat16), 'grp')  38.8 us
    unnamed x146, local copies, waits for them, and re-layouts  28.2 us
    sub x4, matrix products, on_device(): probs_full = jnp.exp(scores - jnp.max(scores, axis=2, keepdims=True))  22 us
  transfers between devices with their start and end apart: 6, of which 4 were waited for; matrix products, arithmetic and copies ran while one was open for 15% of the time, Pallas kernels for 0%

commit v1 on v0

--- a/solution.py
+++ b/solution.py
@@ -182,7 +182,9 @@
     output_first_gradient = lax.psum(
         (adapter_scale * row_contrib).astype(jnp.bfloat16), "grp"
     ).astype(jnp.float32)
-    output_second_gradient = lax.psum(adapter_scale * column_contrib, ("grp", "dev"))
+    x = adapter_scale * column_contrib
+    terms = lax.all_gather(x, ("grp", "dev"), axis=0, tiled=False)
+    output_second_gradient = terms.sum(axis=0)
     empty = jnp.zeros((piece_len, KVH * HEAD_SIZE), jnp.float32)
     key_term = lax.dynamic_update_slice(empty, grad_key_sum, (0, kv_index * HEAD_SIZE))
     value_term = lax.dynamic_update_slice(empty, grad_value_sum, (0, kv_index * HEAD_SIZE))

time: 727 us -> 960 us (1.32)
  waiting for transfers between devices: 391 us -> 616 us
  other arithmetic: 45.6 us -> 63.7 us
    all_gather x0 -> x1, waiting for transfers between devices: none -> 370 us  [on_device(): terms = lax.all_gather(x, ('grp', 'dev'), axis=0, tiled=False)]
    psum x1 -> x0, waiting for transfers between devices: 152 us -> none  [on_device(): lax.psum(adapter_scale * column_contrib, ('grp', 'dev'))]
    reduce_scatter x1, waiting for transfers between devices: 42.5 us -> 0.01 us  [on_device(): lax.psum_scatter(value_term.astype(jnp.bfloat16), 'dev', scatter_dimensio...]
    reduce_scatter x1, waiting for transfers between devices: 0.01 us -> 42 us  [on_device(): lax.psum_scatter(key_term.astype(jnp.bfloat16), 'dev', scatter_dimension=...]
    reduce_sum x0 -> x1, other arithmetic: none -> 21.8 us  [on_device(): output_second_gradient = terms.sum(axis=0)]
    all_to_all x1, starting transfers between devices: 12.4 us -> 23.5 us  [on_device(): lax.all_to_all(outgoing, ('grp', 'dev'), split_axis=0, concat_axis=0, til...]
    unnamed x146 -> x135, local copies, waits for them, and re-layouts: 28.2 us -> 23.9 us
  transfers between devices with their start and end apart: 6 -> 6, of which waited for: 4 -> 5; matrix products, arithmetic and copies ran while one was open for 15% -> 11% of each run, Pallas kernels for 0% -> 0%
where the time goes in v1:
time: 960 us; the launch traced here: 952 us
  waiting for transfers between devices  616 us (64%)
  matrix products  102 us (11%)
  local copies, waits for them, and re-layouts  80.1 us (8%)
  other arithmetic  63.7 us (7%)
  starting transfers between devices  39.3 us (4%)
  blocking collectives  34.9 us (4%)
  between operations  15 us (2%)
    all_gather x1, waiting for transfers between devices, on_device(): terms = lax.all_gather(x, ('grp', 'dev'), axis=0, tiled=False)  370 us
    all_to_all x1, waiting for transfers between devices, on_device(): lax.all_to_all(grad_rows.reshape(experts, capacity, model_width), ('grp',...  101 us
    all_to_all x1, waiting for transfers between devices, on_device(): lax.all_to_all(outgoing, ('grp', 'dev'), split_axis=0, concat_axis=0, til...  94.9 us
    reduce_scatter x1, waiting for transfers between devices, on_device(): lax.psum_scatter(key_term.astype(jnp.bfloat16), 'dev', scatter_dimension=...  42 us
    dot_general x11, matrix products, contraction(): lax.dot_general(left, right, (((left_dim,), (right_dim,)), ((), ())), pre...  36.5 us
    psum x1, blocking collectives, on_device(): lax.psum((adapter_scale * row_contrib).astype(jnp.bfloat16), 'grp')  34.9 us
    unnamed x135, local copies, waits for them, and re-layouts  23.9 us
    all_to_all x1, starting transfers between devices, on_device(): lax.all_to_all(outgoing, ('grp', 'dev'), split_axis=0, concat_axis=0, til...  23.5 us
  transfers between devices with their start and end apart: 6, of which 5 were waited for; matrix products, arithmetic and copies ran while one was open for 11% of the time, Pallas kernels for 0%

profile of v1, /device:TPU:1, one launch (start us, length us, event | category | flops | bytes accessed | tf_op | source)
XLA Modules:
  0.0 951.7 jit_solution(671298067243799853)
XLA Ops:
  10.2 1.1 broadcast_add_fusion
  12.3 2.1 convert_element_type.174
  14.6 1.4 fusion.100
  16.1 10.5 %scatter_custom_fusion = bf16[1280,2048]{1,0:T(8,128)(2,1)} fusion(s32[1024]{0:T(1024)S(1)} %bitcast.380, f32[128,2048]{1,0:T(8,128)} %convert_element_type.174, f32[1024]{0:T(1024)S(1)} %mul.209, bf16[]{:T(256)} %constant.250.clone.1), kind=kCustom, calls=%fused_computation.28 | custom fusion | flops 4194304 | bytes 6295554 | tf_op jit(solution)/shard_map/scatter | solution.py:78
  26.5 9.5 %reshape.411 = bf16[128,10,2048]{2,1,0:T(8,128)(2,1)} reshape(bf16[1280,2048]{1,0:T(8,128)(2,1)} %scatter_custom_fusion) | data formatting | bytes 10485760 | tf_op jit(solution)/shard_map/reshape | solution.py:79
  36.1 23.5 %all-to-all-start = ((bf16[128,10,2048]{2,1,0:T(8,128)(2,1)}), bf16[128,10,2048]{2,1,0:T(8,128)(2,1)}, u32[]{:S(2)}, u32[]{:S(2)}) async-start(bf16[128,10,2048]{2,1,0:T(8,128)(2,1)} %reshape.411), calls=%async_computation | async-start | bytes 16777216 | tf_op jit(solution)/shard_map/all_to_all | solution.py:80
  59.6 6.3 copy.100
  65.9 94.9 %all-to-all-done = bf16[128,10,2048]{2,1,0:T(8,128)(2,1)} async-done(((bf16[128,10,2048]{2,1,0:T(8,128)(2,1)}), bf16[128,10,2048]{2,1,0:T(8,128)(2,1)}, u32[]{:S(2)}, u32[]{:S(2)}) %all-to-all-start) | async-done | bytes 5242912 | tf_op jit(solution)/shard_map/all_to_all | solution.py:80
  160.8 9.8 %reshape.412 = bf16[1280,2048]{1,0:T(8,128)(2,1)} reshape(bf16[128,10,2048]{2,1,0:T(8,128)(2,1)} %all-to-all-done) | data formatting | bytes 10485760 | tf_op jit(solution)/shard_map/reshape | solution.py:81
  170.6 4.3 convolution_convert_fusion.3
  175.0 4.3 fusion.35
  179.4 3.8 fusion.24
  183.2 10.2 %convolution_convert_fusion = bf16[1280,2048]{1,0:T(8,128)(2,1)} fusion(bf16[1,2048,1536]{2,1,0:T(8,128)(2,1)S(1)} %bitcast.383, bf16[1280,768]{0,1:T(8,128)(2,1)S(1)} %get-tuple-element.149, bf16[1280,768]{0,1:T(8,128)(2,1)S(1)} %get-tuple-element.148), kind=kOutput, calls=%fused_computation.14 | convolution fusion | flops 8063549440 | bytes 15466496 | tf_op jit(solution)/shard_map/dot_general | solution.py:14
  193.4 9.5 %reshape.413 = bf16[128,10,2048]{2,1,0:T(8,128)(2,1)} reshape(bf16[1280,2048]{1,0:T(8,128)(2,1)} %convolution_convert_fusion) | data formatting | bytes 10485760 | tf_op jit(solution)/shard_map/reshape | solution.py:91
  202.9 15.0 %all-to-all-start.1 = ((bf16[128,10,2048]{2,1,0:T(8,128)(2,1)}), bf16[128,10,2048]{2,1,0:T(8,128)(2,1)}, u32[]{:S(2)}, u32[]{:S(2)}) async-start(bf16[128,10,2048]{2,1,0:T(8,128)(2,1)} %reshape.413), calls=%async_computation.1 | async-start | bytes 16777216 | tf_op jit(solution)/shard_map/all_to_all | solution.py:90
  218.0 101.3 %all-to-all-done.1 = bf16[128,10,2048]{2,1,0:T(8,128)(2,1)} async-done(((bf16[128,10,2048]{2,1,0:T(8,128)(2,1)}), bf16[128,10,2048]{2,1,0:T(8,128)(2,1)}, u32[]{:S(2)}, u32[]{:S(2)}) %all-to-all-start.1) | async-done | bytes 5242912 | tf_op jit(solution)/shard_map/all_to_all | solution.py:90
  319.3 9.8 %reshape.414 = bf16[1280,2048]{1,0:T(8,128)(2,1)} reshape(bf16[128,10,2048]{2,1,0:T(8,128)(2,1)} %all-to-all-done.1) | data formatting | bytes 10485760 | tf_op jit(solution)/shard_map/reshape | solution.py:97
  329.1 12.0 %gather_fusion = bf16[1024,2048]{1,0:T(8,128)(2,1)} fusion(bf16[1280,2048]{1,0:T(8,128)(2,1)} %reshape.414, s32[1024]{0:T(1024)S(1)} %broadcast_clamp_fusion), kind=kCustom, calls=%fused_computation | custom fusion | bytes 8392704 | tf_op jit(solution)/shard_map/gather | solution.py:97
  341.1 5.1 convert_reduce_fusion
  347.6 1.1 constant_dynamic-slice_fusion
  349.7 1.2 copy.185
  353.5 3.2 fusion.176
  356.7 4.7 fusion.177
  361.4 3.1 fusion.67
  364.5 1.4 convolution_convert_fusion.5
  366.5 6.1 fusion.178
  372.6 3.8 fusion.43
  376.5 1.3 convolution_convert_fusion.4
  378.2 1.3 fusion.96
  379.5 1.9 iota_compare_fusion
  381.4 8.2 fusion.179
  389.6 4.7 fusion.33
  394.3 2.1 copy-done.2
  397.1 8.1 all-gather.4.cloned.1.call-done
  405.3 6.2 convolution_convert_fusion.2
  411.5 2.4 fusion.184
  419.5 1.5 fusion.53
  421.0 1.3 copy-done.11
  422.6 2.5 multiply_reduce_fusion.3
  425.2 2.3 fusion.62
  431.4 1.0 fusion.9
  434.7 1.2 fusion.5
  436.0 1.8 broadcast_in_dim.100.clone
  438.6 2.2 fusion.46
  440.9 1.1 fusion.83
  442.0 1.1 fusion.81
  443.3 1.1 fusion.85
  444.4 2.1 fusion.59
  446.5 2.1 convolution_add_fusion.2
  448.6 2.1 convolution_add_fusion.1
  450.7 2.9 fusion.55
  453.6 3.1 fusion.86
  456.7 5.3 fusion.54
  462.0 1.6 fusion.69
  463.6 2.3 fusion.74
  466.0 1.6 fusion.68
  467.6 1.8 fusion.73
  469.7 1.8 copy.142
  472.3 34.9 %psum.7 = bf16[64,256]{1,0:T(8,128)(2,1)S(1)} all-reduce(bf16[64,256]{1,0:T(8,128)(2,1)S(1)} %fusion.88), channel_id=1, replica_groups=mesh['grp'=8,'dev'=16] {'grp'}, use_global_device_ids=true, to_apply=%region_13.14 | all-reduce | flops 16384 | bytes 65536 | tf_op jit(solution)/shard_map/psum | solution.py:182
  507.8 1.6 convert_element_type.224
  509.5 42.0 %reduce-scatter.3.cloned.1.call-done = bf16[128,512]{1,0:T(8,128)(2,1)} async-done(((bf16[2048,512]{1,0:T(8,128)(2,1)}), bf16[128,512]{1,0:T(8,128)(2,1)}) %reduce-scatter.3.cloned.1.call-update) | async-done | bytes 131088 | tf_op jit(solution)/shard_map/reduce_scatter | solution.py:192
  551.4 1.6 convert_element_type.222
  553.1 370.1 %all-gather.6.cloned.1.call-done = f32[8192,2048]{1,0:T(8,128)} async-done(((f32[64,2048]{1,0:T(8,128)}), f32[8192,2048]{1,0:T(8,128)}) %all-gather.6.cloned.1.call-update) | async-done | bytes 67108880 | tf_op jit(solution)/shard_map/all_gather | solution.py:186
  923.2 21.8 %reduce_sum.148 = f32[64,2048]{1,0:T(8,128)} reduce(f32[128,64,2048]{2,1,0:T(8,128)} %bitcast.38, f32[]{:T(128)} %constant.256.clone.1), dimensions={0}, to_apply=%region_18.19 | reduce | flops 16646144 | bytes 67633152 | tf_op jit(solution)/shard_map/reduce_sum | solution.py:187
  (187 shorter events, 25.7 us)
Async XLA Ops:
  7.2 167.8 %copy-start = (bf16[1,768,2048]{2,1,0:T(8,128)(2,1)S(1)}, bf16[1,768,2048]{2,1,0:T(8,128)(2,1)}, u32[]{:S(2)}) copy-start(bf16[1,768,2048]{2,1,0:T(8,128)(2,1)} %param.39) | copy-start | bytes 9437188
  7.2 7.3 copy-start.54
  36.1 124.7 %all-to-all-start = ((bf16[128,10,2048]{2,1,0:T(8,128)(2,1)}), bf16[128,10,2048]{2,1,0:T(8,128)(2,1)}, u32[]{:S(2)}, u32[]{:S(2)}) async-start(bf16[128,10,2048]{2,1,0:T(8,128)(2,1)} %reshape.411), calls=%async_computation | async-start | bytes 16777216 | tf_op jit(solution)/shard_map/all_to_all | solution.py:80
  65.9 104.7 %copy-start.51 = (bf16[1,64,2048]{2,1,0:T(8,128)(2,1)S(1)}, bf16[1,64,2048]{2,1,0:T(8,128)(2,1)}, u32[]{:S(2)}) copy-start(bf16[1,64,2048]{2,1,0:T(8,128)(2,1)} %param.41) | copy-start | bytes 786436
  170.6 4.4 copy-start.4
  175.0 4.3 copy-start.50
  175.0 4.3 copy-start.20
  175.0 4.3 copy-start.52
  175.0 8.1 slice-start.4
  179.3 3.8 slice-start.5
  202.9 116.3 %all-to-all-start.1 = ((bf16[128,10,2048]{2,1,0:T(8,128)(2,1)}), bf16[128,10,2048]{2,1,0:T(8,128)(2,1)}, u32[]{:S(2)}, u32[]{:S(2)}) async-start(bf16[128,10,2048]{2,1,0:T(8,128)(2,1)} %reshape.413), calls=%async_computation.1 | async-start | bytes 16777216 | tf_op jit(solution)/shard_map/all_to_all | solution.py:90
  217.9 187.3 %all-gather.4.cloned.1.call-start = ((), (), s32[]{:S(2)}) async-start(), calls=%async_computation.4 | async-start | bytes 8912896 | tf_op jit(solution)/shard_map/all_gather | solution.py:102
  341.1 5.1 copy-start.27
  346.2 2.6 copy-start.36
  347.1 160.7 %reduce-scatter.5.cloned.1.call-start = ((), (), s32[]{:S(2)}) async-start(), calls=%async_computation.6 | async-start | bytes 2228224 | tf_op jit(solution)/shard_map/reduce_scatter | solution.py:195
  348.7 4.8 copy-start.12
  349.7 7.0 copy-start.38
  350.9 10.5 %copy-start.44 = (bf16[512,256]{0,1:T(8,128)(2,1)}, bf16[512,256]{0,1:T(8,128)(2,1)S(1)}, u32[]{:S(2)}) copy-start(bf16[512,256]{0,1:T(8,128)(2,1)S(1)} %copy.185) | copy-start | bytes 786436
  351.1 15.4 %copy-start.32 = (bf16[512,256]{0,1:T(8,128)(2,1)}, bf16[512,256]{0,1:T(8,128)(2,1)S(1)}, u32[]{:S(2)}) copy-start(bf16[512,256]{0,1:T(8,128)(2,1)S(1)} %copy.186) | copy-start | bytes 786436
  352.1 24.3 %copy-start.28 = (bf16[1536,128]{0,1:T(8,128)(2,1)}, bf16[1536,128]{0,1:T(8,128)(2,1)S(1)}, u32[]{:S(2)}) copy-start(bf16[1536,128]{0,1:T(8,128)(2,1)S(1)} %copy.190) | copy-start | bytes 1179652
  352.3 12.2 %copy-start.34 = (bf16[1024,128]{0,1:T(8,128)(2,1)}, bf16[1024,128]{0,1:T(8,128)(2,1)S(1)}, u32[]{:S(2)}) copy-start(bf16[1024,128]{0,1:T(8,128)(2,1)S(1)} %copy.189) | copy-start | bytes 786436
  364.5 8.1 copy-start.8
  376.4 1.8 copy-start.26
  377.7 3.7 copy-start.30
  389.6 6.8 copy-start.13
  394.3 2.1 copy-start.2
  405.3 6.2 copy-start.5
  405.3 6.2 copy-start.55
  411.5 2.4 copy-start.21
  411.5 2.4 copy-start.49
  413.9 2.7 copy-start.9
  414.4 2.9 copy-start.19
  414.5 2.8 copy-start.46
  414.5 2.8 copy-start.47
  414.5 3.8 copy-start.42
  414.5 4.0 copy-start.40
  417.3 2.2 copy-start.3
  419.5 3.1 copy-start.18
  422.3 129.1 %reduce-scatter.3.cloned.1.call-start = ((), (), s32[]{:S(2)}) async-start(), calls=%async_computation.5 | async-start | bytes 2228224 | tf_op jit(solution)/shard_map/reduce_scatter | solution.py:192
  425.1 2.4 copy-start.39
  425.1 3.4 copy-start.16
  425.2 3.4 copy-start.35
  425.2 3.4 copy-start.48
  427.5 3.8 slice-start.2
  428.5 1.5 copy-start.45
  428.5 2.9 slice-start.3
  428.5 2.9 copy-start.29
  428.5 2.8 copy-start.43
  430.1 1.3 copy-start.10
  430.1 4.0 slice-start
  431.4 1.7 copy-start.33
  431.4 3.0 slice-start.1
  433.1 1.6 copy-start.14
  433.1 1.7 copy-start.41
  434.7 3.9 copy-start.31
  436.0 2.6 copy-start.6
  440.8 482.4 %all-gather.6.cloned.1.call-start = ((), (), s32[]{:S(2)}) async-start(), calls=%async_computation.7 | async-start | bytes 67633152 | tf_op jit(solution)/shard_map/all_gather | solution.py:186
  448.6 8.1 copy-start.53
  463.6 3.9 copy-start.7
  469.4 2.0 copy-start.22
  469.4 2.2 copy-start.23
  469.6 1.8 copy-start.37
  469.6 2.2 copy-start.24
  923.2 21.8 %copy-start.1 = (bf16[1,768,2048]{2,1,0:T(8,128)(2,1)S(1)}, bf16[1,768,2048]{2,1,0:T(8,128)(2,1)}, u32[]{:S(2)}) copy-start(bf16[1,768,2048]{2,1,0:T(8,128)(2,1)} %param.39) | copy-start | bytes 9437188
  (4 other events, 4.3 us)
Sparse Core Ops, SparseCore 0:
  347.2 57.9 all-gather.3
  422.5 62.3 reduce-scatter.4
  487.3 64.1 reduce-scatter.2
  553.6 369.5 all-gather.5
